TPU v7x, 256 devices: a whole 4x4x8 slice. The times are simulated.
256 devices in a mesh: rows: 16 (over z, core), cols: 16 (over y, x).
Axes of the slice: x: 4, y: 4, z: 8, core: 2. Of those that a mesh axis runs over, the one named last changes fastest.
Arguments:
- tensor: float32 [32, 2048, 2048], P(None, 'rows', 'cols'), may hold values from -819200 to 819200
- second_init: float32 [2048, 64], P('cols'), may hold values from -6 to 6
- third_init: float32 [32, 64], replicated, may hold values from -6 to 6
Outputs:
- first: float32 [2048, 64], P('rows')
- second: float32 [2048, 64], P('cols')
- third: float32 [32, 64], replicated
All inputs are finite; a program needn't handle non-finite values.
Results may differ from a plain program's by a relative error of at most 0.0003.
Values sent between devices are 32-bit elements; how exact they have to be, the bound alone decides.
No kernel may reach another device: no remote copies, remote signals or barrier semaphores. Data moves between devices by JAX's collectives and lax.ppermute only.
A program may use at most 64 MiB of HBM per device.

v0:
```python
import jax
import jax.numpy as jnp
from jax import lax
from jax.sharding import PartitionSpec as P

ITERS = 5
EPSILON = 1e-05
HIGHEST = lax.Precision.HIGHEST


def solve_right(rhs_rows, system):
    cholesky_low = jnp.linalg.cholesky(system)
    halfway = lax.linalg.triangular_solve(
        cholesky_low, rhs_rows, left_side=False, lower=True, transpose_a=True
    )
    return lax.linalg.triangular_solve(cholesky_low, halfway, left_side=False, lower=True)


def gram_local(factor):
    return jnp.dot(factor.T, factor, precision=HIGHEST, preferred_element_type=jnp.float32)


def settle(raw_share, total_rows):
    squares = lax.psum(jnp.sum(raw_share * raw_share, axis=0), ("rows", "cols"))
    col_scale = jnp.sqrt(squares / total_rows + EPSILON)
    normed = raw_share / col_scale
    gram_whole = lax.psum(gram_local(normed), ("rows", "cols"))
    return (col_scale, gram_whole)


def per_device(tensor, second_init, third_init):
    rows_here = tensor.shape[1]
    cols_here = tensor.shape[2]
    total_first = rows_here * lax.axis_size("rows")
    total_second = cols_here * lax.axis_size("cols")
    share_first = rows_here // lax.axis_size("cols")
    share_second = cols_here // lax.axis_size("rows")
    start_first = lax.axis_index("cols") * share_first
    start_second = lax.axis_index("rows") * share_second
    col_scale, gram_second = settle(
        lax.dynamic_slice_in_dim(second_init, start_second, share_second, 0), total_second
    )
    second = second_init / col_scale
    third = third_init
    gram_third = gram_local(third)
    first = None
    for sweep_index in range(ITERS):
        contract_first = lax.dot_general(
            second,
            tensor,
            (((0,), (2,)), ((), ())),
            precision=HIGHEST,
            preferred_element_type=jnp.float32,
        )
        system_first = gram_third * gram_second
        gram_first = None
        partial_first = jnp.einsum("rki,kr->ir", contract_first, third, precision=HIGHEST)
        mttkrp_first = lax.psum(partial_first, "cols")
        raw_block = solve_right(mttkrp_first, system_first)
        col_scale, gram_first = settle(
            lax.dynamic_slice_in_dim(raw_block, start_first, share_first, 0), total_first
        )
        carried_first = raw_block / col_scale
        contract_second = lax.dot_general(
            carried_first,
            tensor,
            (((0,), (1,)), ((), ())),
            precision=HIGHEST,
            preferred_element_type=jnp.float32,
        )
        partial_second = jnp.einsum("rkj,kr->jr", contract_second, third, precision=HIGHEST)
        outgoing = partial_second
        summed_second = lax.psum(outgoing, "rows")
        first = carried_first
        system_second = gram_third * gram_first
        raw_block = solve_right(summed_second, system_second)
        raw_part = lax.dynamic_slice_in_dim(raw_block, start_second, share_second, 0)
        col_scale, gram_second = settle(raw_part, total_second)
        carried_second = raw_block / col_scale
        partial_third = jnp.einsum("rkj,jr->kr", contract_second, carried_second, precision=HIGHEST)
        outgoing = partial_third
        summed_third = lax.psum(outgoing, ("rows", "cols"))
        second = carried_second
        third = solve_right(summed_third, gram_first * gram_second)
        gram_third = gram_local(third)
    return (first, second, third)


def solution(mesh):
    return jax.shard_map(
        per_device,
        mesh=mesh,
        in_specs=(P(None, "rows", "cols"), P("cols", None), P()),
        out_specs=(P("rows", None), P("cols", None), P()),
        check_vma=False,
    )
```

profile of v0, /device:TPU:1, one launch (start us, length us, event | category | flops | bytes accessed | tf_op | source)
XLA Modules:
  0.0 2455.2 jit_solution(10629154190226435686)
XLA Ops:
  1.7 81.4 %psum.259 = f32[64]{0:T(128)S(1)} all-reduce(f32[64]{0:T(128)S(1)} %multiply_reduce_fusion.10), channel_id=1, replica_groups=mesh['rows'=16,'cols'=16] {'rows','cols'}, use_global_device_ids=true, to_apply=%region_1.0 | all-reduce | flops 64 | bytes 512 | tf_op jit(solution)/shard_map/psum | solution.py:24
  85.1 72.8 %psum.260 = f32[64,64]{0,1:T(8,128)S(1)} all-reduce(f32[64,64]{0,1:T(8,128)S(1)} %fusion.163), channel_id=1, replica_groups=mesh['rows'=16,'cols'=16] {'rows','cols'}, use_global_device_ids=true, to_apply=%region_2.0 | all-reduce | flops 4096 | bytes 32768 | tf_op jit(solution)/shard_map/psum | solution.py:27
  175.8 56.8 %psum.261 = f32[128,64]{0,1:T(8,128)S(1)} all-reduce(f32[128,64]{0,1:T(8,128)S(1)} %bitcast.449), channel_id=1, replica_groups=mesh['rows'=16,'cols'=16] {'cols'}, use_global_device_ids=true, to_apply=%region_5.0 | all-reduce | flops 8192 | bytes 65536 | tf_op jit(solution)/shard_map/psum | solution.py:58
  233.2 86.1 %psum.262 = f32[64]{0:T(128)S(1)} all-reduce(f32[64]{0:T(128)S(1)} %multiply_reduce_fusion.9), channel_id=1, replica_groups=mesh['rows'=16,'cols'=16] {'rows','cols'}, use_global_device_ids=true, to_apply=%region_7.11 | all-reduce | flops 64 | bytes 512 | tf_op jit(solution)/shard_map/psum | solution.py:24
  319.6 73.9 %psum.263 = f32[64,64]{0,1:T(8,128)S(1)} all-reduce(f32[64,64]{0,1:T(8,128)S(1)} %fusion.160), channel_id=1, replica_groups=mesh['rows'=16,'cols'=16] {'rows','cols'}, use_global_device_ids=true, to_apply=%region_8.12 | all-reduce | flops 4096 | bytes 32768 | tf_op jit(solution)/shard_map/psum | solution.py:27
  408.5 44.1 %psum.264 = f32[128,64]{0,1:T(8,128)S(1)} all-reduce(f32[128,64]{0,1:T(8,128)S(1)} %bitcast.450), channel_id=1, replica_groups=mesh['rows'=16,'cols'=16] {'rows'}, use_global_device_ids=true, to_apply=%region_9.13 | all-reduce | flops 8192 | bytes 65536 | tf_op jit(solution)/shard_map/psum | solution.py:73
  453.3 76.4 %psum.265 = f32[64]{0:T(128)S(1)} all-reduce(f32[64]{0:T(128)S(1)} %multiply_reduce_fusion.8), channel_id=1, replica_groups=mesh['rows'=16,'cols'=16] {'rows','cols'}, use_global_device_ids=true, to_apply=%region_11.15 | all-reduce | flops 64 | bytes 512 | tf_op jit(solution)/shard_map/psum | solution.py:24
  532.2 74.2 %all-reduce.4 = (f32[32,64]{0,1:T(8,128)S(1)}, f32[64,64]{0,1:T(8,128)S(1)}) all-reduce(f32[32,64]{0,1:T(8,128)S(1)} %bitcast.444, f32[64,64]{0,1:T(8,128)S(1)} %fusion.157), channel_id=1, replica_groups=mesh['rows'=16,'cols'=16] {'rows','cols'}, use_global_device_ids=true, to_apply=%region_13.17 | all-reduce | flops 6144 | bytes 49152 | tf_op jit(solution)/shard_map/psum | solution.py:82
  635.5 56.8 %psum.268 = f32[128,64]{0,1:T(8,128)S(1)} all-reduce(f32[128,64]{0,1:T(8,128)S(1)} %bitcast.451), channel_id=1, replica_groups=mesh['rows'=16,'cols'=16] {'cols'}, use_global_device_ids=true, to_apply=%region_14.20 | all-reduce | flops 8192 | bytes 65536 | tf_op jit(solution)/shard_map/psum | solution.py:58
  692.9 85.3 %psum.269 = f32[64]{0:T(128)S(1)} all-reduce(f32[64]{0:T(128)S(1)} %multiply_reduce_fusion.7), channel_id=1, replica_groups=mesh['rows'=16,'cols'=16] {'rows','cols'}, use_global_device_ids=true, to_apply=%region_16.22 | all-reduce | flops 64 | bytes 512 | tf_op jit(solution)/shard_map/psum | solution.py:24
  778.5 74.9 %psum.270 = f32[64,64]{0,1:T(8,128)S(1)} all-reduce(f32[64,64]{0,1:T(8,128)S(1)} %fusion.155), channel_id=1, replica_groups=mesh['rows'=16,'cols'=16] {'rows','cols'}, use_global_device_ids=true, to_apply=%region_17.23 | all-reduce | flops 4096 | bytes 32768 | tf_op jit(solution)/shard_map/psum | solution.py:27
  868.3 43.4 %psum.271 = f32[128,64]{0,1:T(8,128)S(1)} all-reduce(f32[128,64]{0,1:T(8,128)S(1)} %bitcast.452), channel_id=1, replica_groups=mesh['rows'=16,'cols'=16] {'rows'}, use_global_device_ids=true, to_apply=%region_18.24 | all-reduce | flops 8192 | bytes 65536 | tf_op jit(solution)/shard_map/psum | solution.py:73
  912.2 76.4 %psum.272 = f32[64]{0:T(128)S(1)} all-reduce(f32[64]{0:T(128)S(1)} %multiply_reduce_fusion.6), channel_id=1, replica_groups=mesh['rows'=16,'cols'=16] {'rows','cols'}, use_global_device_ids=true, to_apply=%region_20.26 | all-reduce | flops 64 | bytes 512 | tf_op jit(solution)/shard_map/psum | solution.py:24
  991.2 74.1 %all-reduce.3 = (f32[32,64]{0,1:T(8,128)S(1)}, f32[64,64]{0,1:T(8,128)S(1)}) all-reduce(f32[32,64]{0,1:T(8,128)S(1)} %bitcast.445, f32[64,64]{0,1:T(8,128)S(1)} %fusion.152), channel_id=1, replica_groups=mesh['rows'=16,'cols'=16] {'rows','cols'}, use_global_device_ids=true, to_apply=%region_22.28 | all-reduce | flops 6144 | bytes 49152 | tf_op jit(solution)/shard_map/psum | solution.py:82
  1094.4 56.8 %psum.275 = f32[128,64]{0,1:T(8,128)S(1)} all-reduce(f32[128,64]{0,1:T(8,128)S(1)} %bitcast.453), channel_id=1, replica_groups=mesh['rows'=16,'cols'=16] {'cols'}, use_global_device_ids=true, to_apply=%region_23.29 | all-reduce | flops 8192 | bytes 65536 | tf_op jit(solution)/shard_map/psum | solution.py:58
  1151.8 85.3 %psum.276 = f32[64]{0:T(128)S(1)} all-reduce(f32[64]{0:T(128)S(1)} %multiply_reduce_fusion.5), channel_id=1, replica_groups=mesh['rows'=16,'cols'=16] {'rows','cols'}, use_global_device_ids=true, to_apply=%region_25.31 | all-reduce | flops 64 | bytes 512 | tf_op jit(solution)/shard_map/psum | solution.py:24
  1237.3 74.7 %psum.277 = f32[64,64]{0,1:T(8,128)S(1)} all-reduce(f32[64,64]{0,1:T(8,128)S(1)} %fusion.150), channel_id=1, replica_groups=mesh['rows'=16,'cols'=16] {'rows','cols'}, use_global_device_ids=true, to_apply=%region_26.32 | all-reduce | flops 4096 | bytes 32768 | tf_op jit(solution)/shard_map/psum | solution.py:27
  1326.9 43.3 %psum.278 = f32[128,64]{0,1:T(8,128)S(1)} all-reduce(f32[128,64]{0,1:T(8,128)S(1)} %bitcast.454), channel_id=1, replica_groups=mesh['rows'=16,'cols'=16] {'rows'}, use_global_device_ids=true, to_apply=%region_27.33 | all-reduce | flops 8192 | bytes 65536 | tf_op jit(solution)/shard_map/psum | solution.py:73
  1370.9 76.4 %psum.279 = f32[64]{0:T(128)S(1)} all-reduce(f32[64]{0:T(128)S(1)} %multiply_reduce_fusion.4), channel_id=1, replica_groups=mesh['rows'=16,'cols'=16] {'rows','cols'}, use_global_device_ids=true, to_apply=%region_29.35 | all-reduce | flops 64 | bytes 512 | tf_op jit(solution)/shard_map/psum | solution.py:24
  1449.8 74.3 %all-reduce.2 = (f32[32,64]{0,1:T(8,128)S(1)}, f32[64,64]{0,1:T(8,128)S(1)}) all-reduce(f32[32,64]{0,1:T(8,128)S(1)} %bitcast.446, f32[64,64]{0,1:T(8,128)S(1)} %fusion.147), channel_id=1, replica_groups=mesh['rows'=16,'cols'=16] {'rows','cols'}, use_global_device_ids=true, to_apply=%region_31.37 | all-reduce | flops 6144 | bytes 49152 | tf_op jit(solution)/shard_map/psum | solution.py:82
  1553.2 56.8 %psum.282 = f32[128,64]{0,1:T(8,128)S(1)} all-reduce(f32[128,64]{0,1:T(8,128)S(1)} %bitcast.455), channel_id=1, replica_groups=mesh['rows'=16,'cols'=16] {'cols'}, use_global_device_ids=true, to_apply=%region_32.38 | all-reduce | flops 8192 | bytes 65536 | tf_op jit(solution)/shard_map/psum | solution.py:58
  1610.6 85.3 %psum.283 = f32[64]{0:T(128)S(1)} all-reduce(f32[64]{0:T(128)S(1)} %multiply_reduce_fusion.3), channel_id=1, replica_groups=mesh['rows'=16,'cols'=16] {'rows','cols'}, use_global_device_ids=true, to_apply=%region_34.40 | all-reduce | flops 64 | bytes 512 | tf_op jit(solution)/shard_map/psum | solution.py:24
  1696.2 74.6 %psum.284 = f32[64,64]{0,1:T(8,128)S(1)} all-reduce(f32[64,64]{0,1:T(8,128)S(1)} %fusion.145), channel_id=1, replica_groups=mesh['rows'=16,'cols'=16] {'rows','cols'}, use_global_device_ids=true, to_apply=%region_35.41 | all-reduce | flops 4096 | bytes 32768 | tf_op jit(solution)/shard_map/psum | solution.py:27
  1785.8 43.4 %psum.285 = f32[128,64]{0,1:T(8,128)S(1)} all-reduce(f32[128,64]{0,1:T(8,128)S(1)} %bitcast.456), channel_id=1, replica_groups=mesh['rows'=16,'cols'=16] {'rows'}, use_global_device_ids=true, to_apply=%region_36.42 | all-reduce | flops 8192 | bytes 65536 | tf_op jit(solution)/shard_map/psum | solution.py:73
  1829.7 76.4 %psum.286 = f32[64]{0:T(128)S(1)} all-reduce(f32[64]{0:T(128)S(1)} %multiply_reduce_fusion.2), channel_id=1, replica_groups=mesh['rows'=16,'cols'=16] {'rows','cols'}, use_global_device_ids=true, to_apply=%region_38.44 | all-reduce | flops 64 | bytes 512 | tf_op jit(solution)/shard_map/psum | solution.py:24
  1908.7 74.2 %all-reduce.1 = (f32[32,64]{0,1:T(8,128)S(1)}, f32[64,64]{0,1:T(8,128)S(1)}) all-reduce(f32[32,64]{0,1:T(8,128)S(1)} %bitcast.447, f32[64,64]{0,1:T(8,128)S(1)} %fusion.142), channel_id=1, replica_groups=mesh['rows'=16,'cols'=16] {'rows','cols'}, use_global_device_ids=true, to_apply=%region_40.46 | all-reduce | flops 6144 | bytes 49152 | tf_op jit(solution)/shard_map/psum | solution.py:82
  2011.9 56.8 %psum.289 = f32[128,64]{0,1:T(8,128)S(1)} all-reduce(f32[128,64]{0,1:T(8,128)S(1)} %bitcast.457), channel_id=1, replica_groups=mesh['rows'=16,'cols'=16] {'cols'}, use_global_device_ids=true, to_apply=%region_41.47 | all-reduce | flops 8192 | bytes 65536 | tf_op jit(solution)/shard_map/psum | solution.py:58
  2069.3 85.3 %psum.290 = f32[64]{0:T(128)S(1)} all-reduce(f32[64]{0:T(128)S(1)} %multiply_reduce_fusion.1), channel_id=1, replica_groups=mesh['rows'=16,'cols'=16] {'rows','cols'}, use_global_device_ids=true, to_apply=%region_43.49 | all-reduce | flops 64 | bytes 512 | tf_op jit(solution)/shard_map/psum | solution.py:24
  2155.0 74.7 %psum.291 = f32[64,64]{0,1:T(8,128)S(1)} all-reduce(f32[64,64]{0,1:T(8,128)S(1)} %fusion.140), channel_id=1, replica_groups=mesh['rows'=16,'cols'=16] {'rows','cols'}, use_global_device_ids=true, to_apply=%region_44.50 | all-reduce | flops 4096 | bytes 32768 | tf_op jit(solution)/shard_map/psum | solution.py:27
  2244.6 43.4 %psum.292 = f32[128,64]{0,1:T(8,128)S(1)} all-reduce(f32[128,64]{0,1:T(8,128)S(1)} %bitcast.458), channel_id=1, replica_groups=mesh['rows'=16,'cols'=16] {'rows'}, use_global_device_ids=true, to_apply=%region_45.51 | all-reduce | flops 8192 | bytes 65536 | tf_op jit(solution)/shard_map/psum | solution.py:73
  2288.5 76.4 %psum.293 = f32[64]{0:T(128)S(1)} all-reduce(f32[64]{0:T(128)S(1)} %multiply_reduce_fusion), channel_id=1, replica_groups=mesh['rows'=16,'cols'=16] {'rows','cols'}, use_global_device_ids=true, to_apply=%region_47.53 | all-reduce | flops 64 | bytes 512 | tf_op jit(solution)/shard_map/psum | solution.py:24
  2367.5 73.9 %all-reduce = (f32[32,64]{0,1:T(8,128)S(1)}, f32[64,64]{0,1:T(8,128)S(1)}) all-reduce(f32[32,64]{0,1:T(8,128)S(1)} %bitcast.448, f32[64,64]{0,1:T(8,128)S(1)} %fusion.138), channel_id=1, replica_groups=mesh['rows'=16,'cols'=16] {'rows','cols'}, use_global_device_ids=true, to_apply=%region_49.55 | all-reduce | flops 6144 | bytes 49152 | tf_op jit(solution)/shard_map/psum | solution.py:82
  (225 shorter events, 244.4 us)
Async XLA Ops:
  0.6 170.5 %copy-start = (f32[32,128,128]{2,1,0:T(8,128)S(1)}, f32[32,128,128]{2,1,0:T(8,128)}, u32[]{:S(2)}) copy-start(f32[32,128,128]{2,1,0:T(8,128)} %param.12) | copy-start | bytes 6291460
  2155.0 89.7 %copy-start.1 = (f32[128,64]{0,1:T(8,128)}, f32[128,64]{0,1:T(8,128)S(1)}, u32[]{:S(2)}) copy-start(f32[128,64]{0,1:T(8,128)S(1)} %broadcast_divide_fusion.1) | copy-start | bytes 98308
  2365.3 89.4 %copy-start.2 = (f32[128,64]{0,1:T(8,128)}, f32[128,64]{0,1:T(8,128)S(1)}, u32[]{:S(2)}) copy-start(f32[128,64]{0,1:T(8,128)S(1)} %broadcast_divide_fusion) | copy-start | bytes 98308
where the time goes:
time: 2470 us; the launch traced here: 2460 us
  blocking collectives  2210 us (89%)
  other arithmetic  185 us (7%)
  matrix products  57.5 us (2%)
    psum x11, blocking collectives, settle(): squares = lax.psum(jnp.sum(raw_share * raw_share, axis=0), ('rows', 'cols'))  891 us
    psum x6, blocking collectives, settle(): gram_whole = lax.psum(gram_local(normed), ('rows', 'cols'))  446 us
    psum x5, blocking collectives, per_device(): summed_third = lax.psum(outgoing, ('rows', 'cols'))  371 us
    psum x5, blocking collectives, per_device(): mttkrp_first = lax.psum(partial_first, 'cols')  284 us
    psum x5, blocking collectives, per_device(): summed_second = lax.psum(outgoing, 'rows')  218 us
    another operation x45, other arithmetic, solve_right(): cholesky_low = jnp.linalg.cholesky(system)  97.8 us
    another operation x30, other arithmetic, solve_right(): lax.linalg.triangular_solve(cholesky_low, halfway, left_side=False, lower...  83.2 us

commit v1 on v0

--- a/solution.py
+++ b/solution.py
@@ -21,7 +21,7 @@
 
 
 def settle(raw_share, total_rows):
-    squares = lax.psum(jnp.sum(raw_share * raw_share, axis=0), ("rows", "cols"))
+    squares = lax.psum(lax.psum(jnp.sum(raw_share * raw_share, axis=0), "cols"), "rows")
     col_scale = jnp.sqrt(squares / total_rows + EPSILON)
     normed = raw_share / col_scale
     gram_whole = lax.psum(gram_local(normed), ("rows", "cols"))

time: 2470 us -> 2320 us (0.939)
  blocking collectives: 2210 us -> 2060 us
    psum x11 -> x22, blocking collectives: 891 us -> 750 us  [the longest x11 424 us: settle(): lax.psum(lax.psum(jnp.sum(raw_share * raw_share, axis=0), 'cols'), 'rows')]
where the time goes in v1:
time: 2320 us; the launch traced here: 2310 us
  blocking collectives  2060 us (89%)
  other arithmetic  185 us (8%)
  matrix products  57.5 us (2%)
    psum x6, blocking collectives, settle(): gram_whole = lax.psum(gram_local(normed), ('rows', 'cols'))  441 us
    psum x11, blocking collectives, settle(): lax.psum(lax.psum(jnp.sum(raw_share * raw_share, axis=0), 'cols'), 'rows')  424 us
    psum x5, blocking collectives, per_device(): summed_third = lax.psum(outgoing, ('rows', 'cols'))  366 us
    psum x11, blocking collectives, settle(): lax.psum(jnp.sum(raw_share * raw_share, axis=0), 'cols')  326 us
    psum x5, blocking collectives, per_device(): mttkrp_first = lax.psum(partial_first, 'cols')  284 us
    psum x5, blocking collectives, per_device(): summed_second = lax.psum(outgoing, 'rows')  222 us
    another operation x45, other arithmetic, solve_right(): cholesky_low = jnp.linalg.cholesky(system)  97.8 us
    another operation x30, other arithmetic, solve_right(): lax.linalg.triangular_solve(cholesky_low, halfway, left_side=False, lower...  83.2 us

profile of v1, /device:TPU:1, one launch (start us, length us, event | category | flops | bytes accessed | tf_op | source)
XLA Modules:
  0.0 2309.6 jit_solution(9156920346139958190)
XLA Ops:
  1.7 34.3 %psum.336 = f32[64]{0:T(128)S(1)} all-reduce(f32[64]{0:T(128)S(1)} %multiply_reduce_fusion.10), channel_id=1, replica_groups=mesh['rows'=16,'cols'=16] {'cols'}, use_global_device_ids=true, to_apply=%region_1.0 | all-reduce | flops 64 | bytes 512 | tf_op jit(solution)/shard_map/psum | solution.py:24
  36.0 33.8 %psum.337 = f32[64]{0:T(128)S(1)} all-reduce(f32[64]{0:T(128)S(1)} %psum.336), channel_id=1, replica_groups=mesh['rows'=16,'cols'=16] {'rows'}, use_global_device_ids=true, to_apply=%region_2.0 | all-reduce | flops 64 | bytes 512 | tf_op jit(solution)/shard_map/psum | solution.py:24
  71.7 72.8 %psum.338 = f32[64,64]{0,1:T(8,128)S(1)} all-reduce(f32[64,64]{0,1:T(8,128)S(1)} %fusion.163), channel_id=1, replica_groups=mesh['rows'=16,'cols'=16] {'rows','cols'}, use_global_device_ids=true, to_apply=%region_3.0 | all-reduce | flops 4096 | bytes 32768 | tf_op jit(solution)/shard_map/psum | solution.py:27
  162.5 56.7 %psum.339 = f32[128,64]{0,1:T(8,128)S(1)} all-reduce(f32[128,64]{0,1:T(8,128)S(1)} %bitcast.449), channel_id=1, replica_groups=mesh['rows'=16,'cols'=16] {'cols'}, use_global_device_ids=true, to_apply=%region_6.0 | all-reduce | flops 8192 | bytes 65536 | tf_op jit(solution)/shard_map/psum | solution.py:58
  248.2 44.7 %psum.341 = f32[64]{0:T(128)S(1)} all-reduce(f32[64]{0:T(128)S(1)} %psum.340), channel_id=1, replica_groups=mesh['rows'=16,'cols'=16] {'rows'}, use_global_device_ids=true, to_apply=%region_9.13 | all-reduce | flops 64 | bytes 512 | tf_op jit(solution)/shard_map/psum | solution.py:24
  293.3 73.8 %psum.342 = f32[64,64]{0,1:T(8,128)S(1)} all-reduce(f32[64,64]{0,1:T(8,128)S(1)} %fusion.160), channel_id=1, replica_groups=mesh['rows'=16,'cols'=16] {'rows','cols'}, use_global_device_ids=true, to_apply=%region_10.14 | all-reduce | flops 4096 | bytes 32768 | tf_op jit(solution)/shard_map/psum | solution.py:27
  382.1 44.9 %psum.343 = f32[128,64]{0,1:T(8,128)S(1)} all-reduce(f32[128,64]{0,1:T(8,128)S(1)} %bitcast.450), channel_id=1, replica_groups=mesh['rows'=16,'cols'=16] {'rows'}, use_global_device_ids=true, to_apply=%region_11.15 | all-reduce | flops 8192 | bytes 65536 | tf_op jit(solution)/shard_map/psum | solution.py:73
  457.4 33.5 %psum.345 = f32[64]{0:T(128)S(1)} all-reduce(f32[64]{0:T(128)S(1)} %psum.344), channel_id=1, replica_groups=mesh['rows'=16,'cols'=16] {'rows'}, use_global_device_ids=true, to_apply=%region_14.18 | all-reduce | flops 64 | bytes 512 | tf_op jit(solution)/shard_map/psum | solution.py:24
  493.4 73.2 %all-reduce.4 = (f32[32,64]{0,1:T(8,128)S(1)}, f32[64,64]{0,1:T(8,128)S(1)}) all-reduce(f32[32,64]{0,1:T(8,128)S(1)} %bitcast.444, f32[64,64]{0,1:T(8,128)S(1)} %fusion.157), channel_id=1, replica_groups=mesh['rows'=16,'cols'=16] {'rows','cols'}, use_global_device_ids=true, to_apply=%region_16.20 | all-reduce | flops 6144 | bytes 49152 | tf_op jit(solution)/shard_map/psum | solution.py:82
  595.8 56.8 %psum.348 = f32[128,64]{0,1:T(8,128)S(1)} all-reduce(f32[128,64]{0,1:T(8,128)S(1)} %bitcast.451), channel_id=1, replica_groups=mesh['rows'=16,'cols'=16] {'cols'}, use_global_device_ids=true, to_apply=%region_17.23 | all-reduce | flops 8192 | bytes 65536 | tf_op jit(solution)/shard_map/psum | solution.py:58
  681.7 44.6 %psum.350 = f32[64]{0:T(128)S(1)} all-reduce(f32[64]{0:T(128)S(1)} %psum.349), channel_id=1, replica_groups=mesh['rows'=16,'cols'=16] {'rows'}, use_global_device_ids=true, to_apply=%region_20.26 | all-reduce | flops 64 | bytes 512 | tf_op jit(solution)/shard_map/psum | solution.py:24
  726.6 73.5 %psum.351 = f32[64,64]{0,1:T(8,128)S(1)} all-reduce(f32[64,64]{0,1:T(8,128)S(1)} %fusion.155), channel_id=1, replica_groups=mesh['rows'=16,'cols'=16] {'rows','cols'}, use_global_device_ids=true, to_apply=%region_21.27 | all-reduce | flops 4096 | bytes 32768 | tf_op jit(solution)/shard_map/psum | solution.py:27
  815.0 44.3 %psum.352 = f32[128,64]{0,1:T(8,128)S(1)} all-reduce(f32[128,64]{0,1:T(8,128)S(1)} %bitcast.452), channel_id=1, replica_groups=mesh['rows'=16,'cols'=16] {'rows'}, use_global_device_ids=true, to_apply=%region_22.28 | all-reduce | flops 8192 | bytes 65536 | tf_op jit(solution)/shard_map/psum | solution.py:73
  889.6 33.5 %psum.354 = f32[64]{0:T(128)S(1)} all-reduce(f32[64]{0:T(128)S(1)} %psum.353), channel_id=1, replica_groups=mesh['rows'=16,'cols'=16] {'rows'}, use_global_device_ids=true, to_apply=%region_25.31 | all-reduce | flops 64 | bytes 512 | tf_op jit(solution)/shard_map/psum | solution.py:24
  925.7 73.3 %all-reduce.3 = (f32[32,64]{0,1:T(8,128)S(1)}, f32[64,64]{0,1:T(8,128)S(1)}) all-reduce(f32[32,64]{0,1:T(8,128)S(1)} %bitcast.445, f32[64,64]{0,1:T(8,128)S(1)} %fusion.152), channel_id=1, replica_groups=mesh['rows'=16,'cols'=16] {'rows','cols'}, use_global_device_ids=true, to_apply=%region_27.33 | all-reduce | flops 6144 | bytes 49152 | tf_op jit(solution)/shard_map/psum | solution.py:82
  1028.1 56.8 %psum.357 = f32[128,64]{0,1:T(8,128)S(1)} all-reduce(f32[128,64]{0,1:T(8,128)S(1)} %bitcast.453), channel_id=1, replica_groups=mesh['rows'=16,'cols'=16] {'cols'}, use_global_device_ids=true, to_apply=%region_28.34 | all-reduce | flops 8192 | bytes 65536 | tf_op jit(solution)/shard_map/psum | solution.py:58
  1114.0 44.6 %psum.359 = f32[64]{0:T(128)S(1)} all-reduce(f32[64]{0:T(128)S(1)} %psum.358), channel_id=1, replica_groups=mesh['rows'=16,'cols'=16] {'rows'}, use_global_device_ids=true, to_apply=%region_31.37 | all-reduce | flops 64 | bytes 512 | tf_op jit(solution)/shard_map/psum | solution.py:24
  1158.9 73.7 %psum.360 = f32[64,64]{0,1:T(8,128)S(1)} all-reduce(f32[64,64]{0,1:T(8,128)S(1)} %fusion.150), channel_id=1, replica_groups=mesh['rows'=16,'cols'=16] {'rows','cols'}, use_global_device_ids=true, to_apply=%region_32.38 | all-reduce | flops 4096 | bytes 32768 | tf_op jit(solution)/shard_map/psum | solution.py:27
  1247.5 44.3 %psum.361 = f32[128,64]{0,1:T(8,128)S(1)} all-reduce(f32[128,64]{0,1:T(8,128)S(1)} %bitcast.454), channel_id=1, replica_groups=mesh['rows'=16,'cols'=16] {'rows'}, use_global_device_ids=true, to_apply=%region_33.39 | all-reduce | flops 8192 | bytes 65536 | tf_op jit(solution)/shard_map/psum | solution.py:73
  1322.2 33.5 %psum.363 = f32[64]{0:T(128)S(1)} all-reduce(f32[64]{0:T(128)S(1)} %psum.362), channel_id=1, replica_groups=mesh['rows'=16,'cols'=16] {'rows'}, use_global_device_ids=true, to_apply=%region_36.42 | all-reduce | flops 64 | bytes 512 | tf_op jit(solution)/shard_map/psum | solution.py:24
  1358.2 73.2 %all-reduce.2 = (f32[32,64]{0,1:T(8,128)S(1)}, f32[64,64]{0,1:T(8,128)S(1)}) all-reduce(f32[32,64]{0,1:T(8,128)S(1)} %bitcast.446, f32[64,64]{0,1:T(8,128)S(1)} %fusion.147), channel_id=1, replica_groups=mesh['rows'=16,'cols'=16] {'rows','cols'}, use_global_device_ids=true, to_apply=%region_38.44 | all-reduce | flops 6144 | bytes 49152 | tf_op jit(solution)/shard_map/psum | solution.py:82
  1460.6 56.8 %psum.366 = f32[128,64]{0,1:T(8,128)S(1)} all-reduce(f32[128,64]{0,1:T(8,128)S(1)} %bitcast.455), channel_id=1, replica_groups=mesh['rows'=16,'cols'=16] {'cols'}, use_global_device_ids=true, to_apply=%region_39.45 | all-reduce | flops 8192 | bytes 65536 | tf_op jit(solution)/shard_map/psum | solution.py:58
  1546.5 44.6 %psum.368 = f32[64]{0:T(128)S(1)} all-reduce(f32[64]{0:T(128)S(1)} %psum.367), channel_id=1, replica_groups=mesh['rows'=16,'cols'=16] {'rows'}, use_global_device_ids=true, to_apply=%region_42.48 | all-reduce | flops 64 | bytes 512 | tf_op jit(solution)/shard_map/psum | solution.py:24
  1591.4 73.5 %psum.369 = f32[64,64]{0,1:T(8,128)S(1)} all-reduce(f32[64,64]{0,1:T(8,128)S(1)} %fusion.145), channel_id=1, replica_groups=mesh['rows'=16,'cols'=16] {'rows','cols'}, use_global_device_ids=true, to_apply=%region_43.49 | all-reduce | flops 4096 | bytes 32768 | tf_op jit(solution)/shard_map/psum | solution.py:27
  1679.8 44.3 %psum.370 = f32[128,64]{0,1:T(8,128)S(1)} all-reduce(f32[128,64]{0,1:T(8,128)S(1)} %bitcast.456), channel_id=1, replica_groups=mesh['rows'=16,'cols'=16] {'rows'}, use_global_device_ids=true, to_apply=%region_44.50 | all-reduce | flops 8192 | bytes 65536 | tf_op jit(solution)/shard_map/psum | solution.py:73
  1754.4 33.5 %psum.372 = f32[64]{0:T(128)S(1)} all-reduce(f32[64]{0:T(128)S(1)} %psum.371), channel_id=1, replica_groups=mesh['rows'=16,'cols'=16] {'rows'}, use_global_device_ids=true, to_apply=%region_47.53 | all-reduce | flops 64 | bytes 512 | tf_op jit(solution)/shard_map/psum | solution.py:24
  1790.5 73.5 %all-reduce.1 = (f32[32,64]{0,1:T(8,128)S(1)}, f32[64,64]{0,1:T(8,128)S(1)}) all-reduce(f32[32,64]{0,1:T(8,128)S(1)} %bitcast.447, f32[64,64]{0,1:T(8,128)S(1)} %fusion.142), channel_id=1, replica_groups=mesh['rows'=16,'cols'=16] {'rows','cols'}, use_global_device_ids=true, to_apply=%region_49.55 | all-reduce | flops 6144 | bytes 49152 | tf_op jit(solution)/shard_map/psum | solution.py:82
  1893.0 56.8 %psum.375 = f32[128,64]{0,1:T(8,128)S(1)} all-reduce(f32[128,64]{0,1:T(8,128)S(1)} %bitcast.457), channel_id=1, replica_groups=mesh['rows'=16,'cols'=16] {'cols'}, use_global_device_ids=true, to_apply=%region_50.56 | all-reduce | flops 8192 | bytes 65536 | tf_op jit(solution)/shard_map/psum | solution.py:58
  1979.0 44.6 %psum.377 = f32[64]{0:T(128)S(1)} all-reduce(f32[64]{0:T(128)S(1)} %psum.376), channel_id=1, replica_groups=mesh['rows'=16,'cols'=16] {'rows'}, use_global_device_ids=true, to_apply=%region_53.59 | all-reduce | flops 64 | bytes 512 | tf_op jit(solution)/shard_map/psum | solution.py:24
  2024.0 73.4 %psum.378 = f32[64,64]{0,1:T(8,128)S(1)} all-reduce(f32[64,64]{0,1:T(8,128)S(1)} %fusion.140), channel_id=1, replica_groups=mesh['rows'=16,'cols'=16] {'rows','cols'}, use_global_device_ids=true, to_apply=%region_54.60 | all-reduce | flops 4096 | bytes 32768 | tf_op jit(solution)/shard_map/psum | solution.py:27
  2112.3 44.2 %psum.379 = f32[128,64]{0,1:T(8,128)S(1)} all-reduce(f32[128,64]{0,1:T(8,128)S(1)} %bitcast.458), channel_id=1, replica_groups=mesh['rows'=16,'cols'=16] {'rows'}, use_global_device_ids=true, to_apply=%region_55.61 | all-reduce | flops 8192 | bytes 65536 | tf_op jit(solution)/shard_map/psum | solution.py:73
  2223.0 73.1 %all-reduce = (f32[32,64]{0,1:T(8,128)S(1)}, f32[64,64]{0,1:T(8,128)S(1)}) all-reduce(f32[32,64]{0,1:T(8,128)S(1)} %bitcast.448, f32[64,64]{0,1:T(8,128)S(1)} %fusion.138), channel_id=1, replica_groups=mesh['rows'=16,'cols'=16] {'rows','cols'}, use_global_device_ids=true, to_apply=%region_60.66 | all-reduce | flops 6144 | bytes 49152 | tf_op jit(solution)/shard_map/psum | solution.py:82
  (236 shorter events, 569.8 us)
Async XLA Ops:
  0.6 157.1 %copy-start = (f32[32,128,128]{2,1,0:T(8,128)S(1)}, f32[32,128,128]{2,1,0:T(8,128)}, u32[]{:S(2)}) copy-start(f32[32,128,128]{2,1,0:T(8,128)} %param.12) | copy-start | bytes 6291460
  2023.9 88.4 %copy-start.1 = (f32[128,64]{0,1:T(8,128)}, f32[128,64]{0,1:T(8,128)S(1)}, u32[]{:S(2)}) copy-start(f32[128,64]{0,1:T(8,128)S(1)} %broadcast_divide_fusion.1) | copy-start | bytes 98308
  2220.8 88.5 %copy-start.2 = (f32[128,64]{0,1:T(8,128)}, f32[128,64]{0,1:T(8,128)S(1)}, u32[]{:S(2)}) copy-start(f32[128,64]{0,1:T(8,128)S(1)} %broadcast_divide_fusion) | copy-start | bytes 98308
